TPU v7x, 256 devices: a whole 4x4x8 slice. The times are simulated.
256 devices in a mesh: row: 16 (over y, x), col: 16 (over z, core).
Axes of the slice: x: 4, y: 4, z: 8, core: 2. Of those that a mesh axis runs over, the one named last changes fastest.
Arguments:
- fitting: bfloat16 [512, 512, 256], P(('row', 'col')), may hold values from -6 to 6
- coefficients: bfloat16 [64, 64, 6, 256, 128], P('row', 'col'), may hold values from -0.375 to 0.375
- amplitudes: bfloat16 [64, 64, 4096], P('row', 'col'), may hold values from -6 to 6
- intersections: bfloat16 [64, 64, 8, 4096], P('row', 'col'), may hold values from -0.33 to 1.33
- virtual_energy: float32 [64, 64, 64], P('row', 'col'), may hold values from 0.2 to 2
- occupied_energy: float32 [64], replicated, may hold values from -1.5 to -0.3
- kept_count: int32 [64, 64], P('row', 'col'), may hold values from 16 to 64
- orbital_atoms: int32 [64, 3], replicated, may hold values from 0 to 511, as said below
- fock_partner: int32 [64, 4], replicated, may hold values from 0 to 63, as said below
- fock_value: float32 [64, 4], replicated, may hold values from -3 to 3
Outputs:
- residual: float32 [64, 64, 4096], P('row', 'col')
Inputs may be any that keep to these rules, and one draw needn't show every extreme that they name: `orbital_atoms`: the 3 atoms of orbital i are different and lie in [(i // 4) * 32, (i // 4 + 1) * 32). fock_partner[i, n] differs from i by at most 4.
All inputs are finite; a program needn't handle non-finite values.
Results may differ from a plain program's by a relative error of at most 0.0029.
Values may be sent and summed in bfloat16 or wider, within the bound.
A program may use at most 128 MiB of HBM per device.

v0:
```python
import jax
import jax.numpy as jnp
from jax import lax
from jax.sharding import PartitionSpec as P

AUX = 512
NPNO = 64
DOMAIN = 3
PARTNERS = 4


def from_root(value, axis, source):
    kept = jnp.where(lax.axis_index(axis) == source, value, 0).astype(value.dtype)
    return lax.psum(kept, axis)


def passed_along(block, axis, distance):
    devices = range(lax.axis_size(axis))
    route = [(i - distance, i) for i in devices if i - distance in devices]
    return lax.ppermute(block, axis, route)


def on_device(
    fitting,
    coefficients,
    amplitudes,
    intersections,
    virtual_energy,
    occupied_energy,
    kept_count,
    orbital_atoms,
    fock_partner,
    fock_value,
):
    row_count = amplitudes.shape[0]
    column_count = amplitudes.shape[1]
    domain_size = orbital_atoms.shape[1]
    row_place = lax.axis_index("row")
    column_place = lax.axis_index("col")
    row_atoms = fitting.shape[0] * lax.axis_size("col")
    first_row = row_place * row_count
    first_column = column_place * column_count
    wanted = (
        lax.dynamic_slice_in_dim(orbital_atoms, first_row, row_count, 0) - row_place * row_atoms
    )
    piece = lax.all_gather(fitting, "col", axis=0, tiled=True)
    labels = jnp.arange(piece.shape[0], dtype=jnp.int32)
    picker = (wanted[:, :, None] == labels[None, None, :]).astype(jnp.bfloat16)
    added = jnp.einsum("ism,map->isap", picker, piece, preferred_element_type=jnp.float32)
    row_fit = added.astype(jnp.bfloat16)
    source_row = first_column // row_count
    column_fit = from_root(row_fit, "row", source_row)
    own_side = jnp.einsum(
        "isap,ijspq->ijsaq",
        row_fit,
        coefficients[:, :, :domain_size],
        preferred_element_type=jnp.float32,
    ).astype(jnp.bfloat16)
    other_side = jnp.einsum(
        "jsap,ijspq->ijsaq",
        column_fit,
        coefficients[:, :, domain_size:],
        preferred_element_type=jnp.float32,
    ).astype(jnp.bfloat16)
    exchange_part = jnp.einsum(
        "ijsaq,ijsar->ijqr",
        own_side[..., :NPNO],
        own_side[..., NPNO:],
        preferred_element_type=jnp.float32,
    )
    exchange_part = exchange_part + jnp.einsum(
        "ijsaq,ijsar->ijqr",
        other_side[..., :NPNO],
        other_side[..., NPNO:],
        preferred_element_type=jnp.float32,
    )
    exchange_part = exchange_part * (2 * DOMAIN * AUX) ** (-0.5)
    row_partner = lax.dynamic_slice_in_dim(fock_partner, first_row, row_count, 0)
    column_partner = lax.dynamic_slice_in_dim(fock_partner, first_column, column_count, 0)
    below_rows = passed_along(amplitudes, "row", 1)
    above_rows = passed_along(amplitudes, "row", -1)
    row_source = jnp.concatenate([below_rows, amplitudes, above_rows], axis=0)
    below_columns = passed_along(amplitudes, "col", 1)
    above_columns = passed_along(amplitudes, "col", -1)
    column_source = jnp.concatenate([below_columns, amplitudes, above_columns], axis=1)
    row_pick = row_partner - (first_row - column_count)
    column_pick = column_partner - (first_column - column_count)
    from_rows = jnp.transpose(jnp.take(row_source, row_pick, axis=0), (0, 2, 1, 3))
    from_columns = jnp.take(column_source, column_pick, axis=1)
    partners = jnp.concatenate([from_rows, from_columns], axis=2).reshape(
        row_count, column_count, 2 * PARTNERS, NPNO, NPNO
    )
    intersection_mats = intersections.reshape(row_count, column_count, 2 * PARTNERS, NPNO, NPNO)
    half = jnp.einsum(
        "ijnab,ijnbc->ijnac", intersection_mats, partners, preferred_element_type=jnp.float32
    ).astype(jnp.bfloat16)
    sandwich = jnp.einsum(
        "ijnac,ijndc->ijnad", half, intersection_mats, preferred_element_type=jnp.float32
    )
    row_weight = lax.dynamic_slice_in_dim(fock_value, first_row, row_count, 0)
    column_weight = lax.dynamic_slice_in_dim(fock_value, first_column, column_count, 0)
    weights = jnp.concatenate(
        [
            jnp.broadcast_to(row_weight[:, None, :], (row_count, column_count, PARTNERS)),
            jnp.broadcast_to(column_weight[None, :, :], (row_count, column_count, PARTNERS)),
        ],
        axis=2,
    )
    coupling = jnp.einsum("ijn,ijnad->ijad", weights, sandwich)
    row_occupied = lax.dynamic_slice_in_dim(occupied_energy, first_row, row_count, 0)
    column_occupied = lax.dynamic_slice_in_dim(occupied_energy, first_column, column_count, 0)
    shift = (
        virtual_energy[:, :, :, None]
        + virtual_energy[:, :, None, :]
        - row_occupied[:, None, None, None]
        - column_occupied[None, :, None, None]
    )
    current = amplitudes.reshape(row_count, column_count, NPNO, NPNO).astype(jnp.float32)
    result = exchange_part + shift * current - coupling
    levels = jnp.arange(NPNO, dtype=jnp.int32)
    count = kept_count[:, :, None, None]
    keep = (levels[None, None, :, None] < count) & (levels[None, None, None, :] < count)
    masked = jnp.where(keep, result, jnp.zeros_like(result))
    return masked.reshape(row_count, column_count, NPNO * NPNO)


def solution(mesh):
    placed = (
        P(("row", "col"), None, None),
        P("row", "col", None, None, None),
        P("row", "col", None),
        P("row", "col", None, None),
        P("row", "col", None),
        P(),
        P("row", "col"),
        P(),
        P(),
        P(),
    )
    return jax.shard_map(
        on_device, mesh=mesh, in_specs=placed, out_specs=P("row", "col", None), check_vma=False
    )
```

profile of v0, /device:TPU:1, one launch (start us, length us, event | category | flops | bytes accessed | tf_op | source)
XLA Modules:
  0.0 198.9 jit_solution(497864777100827050)
XLA Ops:
  6.5 0.7 all-gather.2.cloned.1.call-update
  7.3 0.0 all-reduce.2.cloned.1.call-start
  7.3 1.0 copy.82
  8.3 4.9 %collective-permute-start.2 = (bf16[4,4,4096]{2,0,1:T(4,128)(2,1)S(1)}, bf16[4,4,4096]{2,0,1:T(4,128)(2,1)S(1)}, u32[]{:S(2)}, u32[]{:S(2)}) collective-permute-start(bf16[4,4,4096]{2,0,1:T(4,128)(2,1)S(1)} %copy.82), channel_id=1, source_target_pairs={{0,1},{1,2},{2,3},{3,4},{4,5},{5,6},{6,7},{7,8},{8,9},{9,10},{10,1... | collective-permute-start | bytes 393224 | tf_op jit(solution)/shard_map/ppermute | solution.py:20
  13.2 1.9 collective-permute-start.3
  15.2 3.1 %collective-permute-start = (bf16[4,4,4096]{2,1,0:T(4,128)(2,1)}, bf16[4,4,4096]{2,1,0:T(4,128)(2,1)S(1)}, u32[]{:S(2)}, u32[]{:S(2)}) collective-permute-start(bf16[4,4,4096]{2,1,0:T(4,128)(2,1)} %param.12), channel_id=1, source_target_pairs={{0,16},{16,32},{32,48},{48,64},{64,80},{80,96},{96,112},{112,128},... | collective-permute-start | bytes 393224 | tf_op jit(solution)/shard_map/ppermute | solution.py:20
  18.3 1.3 collective-permute-start.1
  19.6 0.8 compare_and_fusion.1
  20.5 0.1 copy.85
  20.6 0.1 reshape.58
  20.6 0.1 copy.79
  20.7 0.1 reshape.50
  20.8 0.8 dynamic-slice_subtract_fusion
  21.6 0.8 constant_dynamic-slice_fusion.1
  22.4 0.8 iota_compare_fusion
  23.2 6.7 %fusion.63 = (bf16[4,4,3,256,128]{4,3,2,1,0:T(8,128)(2,1)}, bf16[4,4,3,256,128]{4,3,2,1,0:T(8,128)(2,1)}) fusion(bf16[4,4,6,256,128]{4,3,2,1,0:T(8,128)(2,1)} %param.11), kind=kLoop, calls=%fused_computation.53 | loop fusion | bytes 12582912 | tf_op jit(solution)/shard_map/slice | solution.py:62
  29.9 0.1 fusion.65
  30.0 1.0 reshape.47
  31.1 0.1 copy.81
  31.2 0.1 copy.78
  31.3 3.3 %reshape.45 = bf16[4,4,8,64,64]{4,3,2,1,0:T(8,128)(2,1)S(1)} reshape(bf16[4,4,8,4096]{3,2,1,0:T(8,128)(2,1)} %param.13) | data formatting | bytes 2097152 | tf_op jit(solution)/shard_map/reshape | solution.py:93
  34.5 0.1 copy.76
  34.6 0.1 copy.77
  34.7 0.1 pad_maximum_fusion.3
  34.8 0.3 pad_maximum_fusion.2
  35.1 1.0 gather_fusion.1
  36.1 0.3 pad_maximum_fusion.1
  36.4 1.8 gather_fusion
  38.2 1.5 fusion.57
  39.7 29.6 %all-gather.2.cloned.1.call-done = bf16[32,512,256]{2,1,0:T(8,128)(2,1)} async-done(((bf16[2,512,256]{2,1,0:T(8,128)(2,1)}), bf16[32,512,256]{2,1,0:T(8,128)(2,1)}) %all-gather.2.cloned.1.call-update) | async-done | bytes 8388624 | tf_op jit(solution)/shard_map/all_gather | solution.py:46
  69.2 12.0 %broadcast_select_fusion = (bf16[4,3,512,256]{3,0,2,1:T(4,128)(2,1)}, bf16[4,3,512,256]{3,0,2,1:T(4,128)(2,1)}) fusion(pred[]{:T(512)S(6)} %eq.19, bf16[32,512,256]{2,1,0:T(8,128)(2,1)} %all-gather.2.cloned.1.call-done, s32[4,3]{0,1:T(4,128)S(1)} %dynamic-slice_subtract_fusion), kind=kOutput, calls=%fused_computation.19 | convolution fusion | flops 103809408 | bytes 14680113 | tf_op jit(solution)/shard_map/ism,map->isap/dot_general | solution.py:49
  81.2 0.0 all-reduce.2.cloned.1.call-update
  81.2 2.0 pad_maximum_fusion
  83.2 3.3 %reshape.44 = bf16[4,4,8,64,64]{4,3,2,1,0:T(8,128)(2,1)} reshape(bf16[4,4,8,4096]{3,2,1,0:T(8,128)(2,1)S(1)} %pad_maximum_fusion) | data formatting | bytes 2097152 | tf_op jit(solution)/shard_map/reshape | solution.py:90
  86.5 5.3 %fusion.18 = bf16[4,4,8,64,64]{4,3,2,1,0:T(8,128)(2,1)} fusion(bf16[4,4,8,64,64]{4,3,2,1,0:T(8,128)(2,1)S(1)} %reshape.45, bf16[4,4,8,64,64]{4,3,2,1,0:T(8,128)(2,1)} %reshape.44), kind=kOutput, calls=%fused_computation.21 | convolution fusion | flops 134742016 | bytes 3145728 | tf_op jit(solution)/shard_map/ijnac,ijndc->ijnad/dot_general | solution.py:97
  91.8 3.8 %fusion.3 = f32[4,4,1,64,64]{4,2,3,1,0:T(1,128)} fusion(f32[4,4,8,1,1]{2,3,4,1,0:T(1,128)S(1)} %bitcast.64, bf16[4,4,8,64,64]{4,3,2,1,0:T(8,128)(2,1)} %fusion.18), kind=kOutput, calls=%fused_computation.7 | convolution fusion | flops 1048576 | bytes 1311232 | tf_op jit(solution)/shard_map/ijn,ijnad->ijad/dot_general | solution.py:109
  95.6 4.8 %convert_bitcast_fusion.1 = bf16[4,4,3,512,128]{3,4,1,2,0:T(8,128)(2,1)S(1)} fusion(bf16[4,4,3,256,128]{4,3,2,1,0:T(8,128)(2,1)} %get-tuple-element.12, bf16[4,3,512,256,1]{3,0,2,1,4:T(4,128)(2,1)} %bitcast.60), kind=kOutput, calls=%fused_computation.6 | convolution fusion | flops 1613758464 | bytes 12582912 | tf_op jit(solution)/shard_map/isap,ijspq->ijsaq/dot_general | solution.py:53
  100.4 0.8 fusion.64
  101.2 1.7 fusion.22
  103.0 82.1 %all-reduce.2.cloned.1.call-done = bf16[4,3,512,256]{3,0,2,1:T(4,128)(2,1)} async-done(((bf16[4,3,512,256]{3,0,2,1:T(4,128)(2,1)}), bf16[4,3,512,256]{3,0,2,1:T(4,128)(2,1)}) %all-reduce.2.cloned.1.call-update) | async-done | bytes 3145744 | tf_op jit(solution)/shard_map/psum | solution.py:14
  185.1 3.7 %convert_bitcast_fusion = bf16[4,4,3,512,128]{3,4,0,2,1:T(8,128)(2,1)S(1)} fusion(bf16[4,4,3,256,128]{4,3,2,1,0:T(8,128)(2,1)S(1)} %copy-done, bf16[4,3,512,256,1]{3,0,2,1,4:T(4,128)(2,1)} %bitcast.59), kind=kOutput, calls=%fused_computation.5 | convolution fusion | flops 1613758464 | bytes 12582912 | tf_op jit(solution)/shard_map/jsap,ijspq->ijsaq/dot_general | solution.py:59
  188.8 0.0 copy-start.5
  188.8 0.4 fusion.62
  189.3 0.5 copy-done.2
  189.8 0.2 copy-done.3
  190.0 0.2 copy-done.6
  190.2 1.0 fusion.52
  191.2 0.9 reshape.46
  (19 shorter events, 0.0 us)
Async XLA Ops:
  6.5 62.7 %all-gather.2.cloned.1.call-start = ((), (), s32[]{:S(2)}) async-start(), calls=%async_computation | async-start | bytes 8912896 | tf_op jit(solution)/shard_map/all_gather | solution.py:46
  7.3 177.8 %all-reduce.2.cloned.1.call-start = ((), (), s32[]{:S(2)}) async-start(), calls=%async_computation.1 | async-start | bytes 6291456 | tf_op jit(solution)/shard_map/psum | solution.py:14
  8.3 26.5 %collective-permute-start.2 = (bf16[4,4,4096]{2,0,1:T(4,128)(2,1)S(1)}, bf16[4,4,4096]{2,0,1:T(4,128)(2,1)S(1)}, u32[]{:S(2)}, u32[]{:S(2)}) collective-permute-start(bf16[4,4,4096]{2,0,1:T(4,128)(2,1)S(1)} %copy.82), channel_id=1, source_target_pairs={{0,1},{1,2},{2,3},{3,4},{4,5},{5,6},{6,7},{7,8},{8,9},{9,10},{10,1... | collective-permute-start | bytes 393224 | tf_op jit(solution)/shard_map/ppermute | solution.py:20
  13.2 21.6 %collective-permute-start.3 = (bf16[4,4,4096]{2,0,1:T(4,128)(2,1)S(1)}, bf16[4,4,4096]{2,0,1:T(4,128)(2,1)S(1)}, u32[]{:S(2)}, u32[]{:S(2)}) collective-permute-start(bf16[4,4,4096]{2,0,1:T(4,128)(2,1)S(1)} %copy.82), channel_id=1, source_target_pairs={{1,0},{2,1},{3,2},{4,3},{5,4},{6,5},{7,6},{8,7},{9,8},{10,9},{11,1... | collective-permute-start | bytes 393224 | tf_op jit(solution)/shard_map/ppermute | solution.py:20
  15.2 20.9 %collective-permute-start = (bf16[4,4,4096]{2,1,0:T(4,128)(2,1)}, bf16[4,4,4096]{2,1,0:T(4,128)(2,1)S(1)}, u32[]{:S(2)}, u32[]{:S(2)}) collective-permute-start(bf16[4,4,4096]{2,1,0:T(4,128)(2,1)} %param.12), channel_id=1, source_target_pairs={{0,16},{16,32},{32,48},{48,64},{64,80},{80,96},{96,112},{112,128},... | collective-permute-start | bytes 393224 | tf_op jit(solution)/shard_map/ppermute | solution.py:20
  18.3 17.8 %collective-permute-start.1 = (bf16[4,4,4096]{2,1,0:T(4,128)(2,1)}, bf16[4,4,4096]{2,1,0:T(4,128)(2,1)S(1)}, u32[]{:S(2)}, u32[]{:S(2)}) collective-permute-start(bf16[4,4,4096]{2,1,0:T(4,128)(2,1)} %param.12), channel_id=1, source_target_pairs={{16,0},{32,16},{48,32},{64,48},{80,64},{96,80},{112,96},{128,112},... | collective-permute-start | bytes 393224 | tf_op jit(solution)/shard_map/ppermute | solution.py:20
  23.2 6.8 %copy-start.4 = (f32[64]{0:T(128)S(1)}, f32[64]{0:T(128)}, u32[]{:S(2)}) copy-start(f32[64]{0:T(128)} %param.15) | copy-start | bytes 772
  23.2 6.8 %copy-start.1 = (bf16[4,4,4096]{2,1,0:T(4,128)(2,1)S(1)}, bf16[4,4,4096]{2,1,0:T(4,128)(2,1)}, u32[]{:S(2)}) copy-start(bf16[4,4,4096]{2,1,0:T(4,128)(2,1)} %param.12) | copy-start | bytes 393220
  101.2 83.8 %copy-start = (bf16[4,4,3,256,128]{4,3,2,1,0:T(8,128)(2,1)S(1)}, bf16[4,4,3,256,128]{4,3,2,1,0:T(8,128)(2,1)}, u32[]{:S(2)}) copy-start(bf16[4,4,3,256,128]{4,3,2,1,0:T(8,128)(2,1)} %get-tuple-element.11) | copy-start | bytes 9437188
  188.8 1.0 copy-start.2
  188.8 1.2 copy-start.3
  188.8 1.2 copy-start.5
  188.8 1.3 copy-start.6
Sparse Core Ops, SparseCore 0:
  9.2 60.0 all-gather.1
  81.4 103.6 all-reduce.1
where the time goes:
time: 199 us
  waiting for transfers between devices  112 us (56%)
  matrix products  32.4 us (16%)
  local copies, waits for them, and re-layouts  22.8 us (11%)
  between operations  13.6 us (7%)
  starting transfers between devices  11.3 us (6%)
  other arithmetic  6.46 us (3%)
    psum x1, waiting for transfers between devices, from_root(): return lax.psum(kept, axis)  82.1 us
    all_gather x1, waiting for transfers between devices, on_device(): piece = lax.all_gather(fitting, 'col', axis=0, tiled=True)  29.6 us
    dot_general x1, matrix products, on_device(): jnp.einsum('ism,map->isap', picker, piece, preferred_element_type=jnp.flo...  12 us
    ppermute x4, starting transfers between devices, passed_along(): return lax.ppermute(block, axis, route)  11.3 us
    slice x1, local copies, waits for them, and re-layouts, on_device(): coefficients[:, :, domain_size:]  6.75 us
    dot_general x1, matrix products, on_device(): jnp.einsum('ijnac,ijndc->ijnad', half, intersection_mats, preferred_eleme...  5.3 us
    dot_general x1, matrix products, on_device(): jnp.einsum('isap,ijspq->ijsaq', row_fit, coefficients[:, :, :domain_size]...  4.82 us
  transfers between devices with their start and end apart: 6, of which 2 were waited for; matrix products, arithmetic and copies ran while one was open for 21% of the time, Pallas kernels for 0%

commit v1 on v0

--- a/solution.py
+++ b/solution.py
@@ -11,7 +11,7 @@
 
 def from_root(value, axis, source):
     kept = jnp.where(lax.axis_index(axis) == source, value, 0).astype(value.dtype)
-    return lax.psum(kept, axis)
+    return jnp.sum(lax.all_gather(kept, axis_name=axis), 0)
 
 
 def passed_along(block, axis, distance):

time: 199 us -> 400 us (2.01)
  waiting for transfers between devices: 112 us -> 298 us
  other arithmetic: 6.46 us -> 21 us
    all_gather x0 -> x1, waiting for transfers between devices: none -> 236 us  [from_root(): return jnp.sum(lax.all_gather(kept, axis_name=axis), 0)]
    psum x1 -> x0, waiting for transfers between devices: 82.1 us -> none  [from_root(): return lax.psum(kept, axis)]
    all_gather x1, waiting for transfers between devices: 29.6 us -> 61.1 us  [on_device(): piece = lax.all_gather(fitting, 'col', axis=0, tiled=True)]
    reduce_sum x0 -> x1, other arithmetic: none -> 16.9 us  [from_root(): return jnp.sum(lax.all_gather(kept, axis_name=axis), 0)]
  transfers between devices with their start and end apart: 6 -> 6, of which waited for: 2 -> 2; matrix products, arithmetic and copies ran while one was open for 21% -> 10% of each run, Pallas kernels for 0% -> 0%
where the time goes in v1:
time: 400 us
  waiting for transfers between devices  298 us (74%)
  matrix products  29.6 us (7%)
  local copies, waits for them, and re-layouts  26.6 us (7%)
  other arithmetic  21 us (5%)
  between operations  13.7 us (3%)
  starting transfers between devices  11.1 us (3%)
    all_gather x1, waiting for transfers between devices, from_root(): return jnp.sum(lax.all_gather(kept, axis_name=axis), 0)  236 us
    all_gather x1, waiting for transfers between devices, on_device(): piece = lax.all_gather(fitting, 'col', axis=0, tiled=True)  61.1 us
    reduce_sum x1, other arithmetic, from_root(): return jnp.sum(lax.all_gather(kept, axis_name=axis), 0)  16.9 us
    dot_general x1, matrix products, on_device(): jnp.einsum('ism,map->isap', picker, piece, preferred_element_type=jnp.flo...  11.1 us
    ppermute x4, starting transfers between devices, passed_along(): return lax.ppermute(block, axis, route)  11 us
  transfers between devices with their start and end apart: 6, of which 2 were waited for; matrix products, arithmetic and copies ran while one was open for 10% of the time, Pallas kernels for 0%

profile of v1, /device:TPU:1, one launch (start us, length us, event | category | flops | bytes accessed | tf_op | source)
XLA Modules:
  0.0 399.7 jit_solution(14663510709073183754)
XLA Ops:
  6.5 0.7 all-gather.4.cloned.1.call-update
  7.3 0.8 dynamic-slice_subtract_fusion
  8.1 61.1 %all-gather.4.cloned.1.call-done = bf16[32,512,256]{2,1,0:T(8,128)(2,1)} async-done(((bf16[2,512,256]{2,1,0:T(8,128)(2,1)}), bf16[32,512,256]{2,1,0:T(8,128)(2,1)}) %all-gather.4.cloned.1.call-update) | async-done | bytes 8388624 | tf_op jit(solution)/shard_map/all_gather | solution.py:46
  69.2 11.1 %broadcast_select_fusion = (bf16[4,3,512,256]{3,0,2,1:T(4,128)(2,1)S(1)}, bf16[4,3,512,256]{3,0,2,1:T(4,128)(2,1)}) fusion(pred[]{:T(512)S(6)} %eq.19, bf16[32,512,256]{2,1,0:T(8,128)(2,1)} %all-gather.4.cloned.1.call-done, s32[4,3]{0,1:T(4,128)S(1)} %dynamic-slice_subtract_fusion), kind=kOutput, calls=%fused_computation.20 | convolution fusion | flops 103809408 | bytes 14680113 | tf_op jit(solution)/shard_map/ism,map->isap/dot_general | solution.py:49
  80.3 2.1 copy.72
  82.4 0.9 copy-done.1
  83.3 0.1 copy.84
  83.4 2.2 collective-permute-start.3
  85.6 3.4 collective-permute-start.2
  89.0 1.3 collective-permute-start.1
  90.3 4.2 %collective-permute-start = (bf16[4,4,4096]{2,1,0:T(4,128)(2,1)S(1)}, bf16[4,4,4096]{2,1,0:T(4,128)(2,1)S(1)}, u32[]{:S(2)}, u32[]{:S(2)}) collective-permute-start(bf16[4,4,4096]{2,1,0:T(4,128)(2,1)S(1)} %copy-done.1), channel_id=1, source_target_pairs={{0,16},{16,32},{32,48},{48,64},{64,80},{80,96},{96,112},{112,128},... | collective-permute-start | bytes 393224 | tf_op jit(solution)/shard_map/ppermute | solution.py:20
  94.5 0.1 compare_and_fusion.1
  94.6 0.1 copy.81
  94.7 0.1 reshape.50
  94.7 0.1 copy.87
  94.8 0.1 reshape.58
  95.0 0.1 iota_compare_fusion
  95.1 7.1 %fusion.63 = (bf16[4,4,3,256,128]{4,3,2,1,0:T(8,128)(2,1)}, bf16[4,4,3,256,128]{4,3,2,1,0:T(8,128)(2,1)}) fusion(bf16[4,4,6,256,128]{4,3,2,1,0:T(8,128)(2,1)} %param.11), kind=kLoop, calls=%fused_computation.54 | loop fusion | bytes 12582912 | tf_op jit(solution)/shard_map/slice | solution.py:62
  102.2 0.1 fusion.65
  102.3 1.0 reshape.47
  103.4 0.1 copy.80
  103.5 0.1 copy.83
  103.6 0.1 copy.78
  103.7 0.1 copy.79
  103.8 3.3 reshape.45
  107.0 0.1 pad_maximum_fusion.3
  107.1 0.3 pad_maximum_fusion.2
  107.4 1.0 gather_fusion.1
  108.4 0.3 pad_maximum_fusion.1
  108.7 1.8 gather_fusion
  110.5 0.7 fusion.57
  111.2 1.8 pad_maximum_fusion
  113.0 3.3 reshape.44
  116.3 5.3 %fusion.18 = bf16[4,4,8,64,64]{4,3,2,1,0:T(8,128)(2,1)} fusion(bf16[4,4,8,64,64]{4,3,2,1,0:T(8,128)(2,1)S(1)} %reshape.45, bf16[4,4,8,64,64]{4,3,2,1,0:T(8,128)(2,1)} %reshape.44), kind=kOutput, calls=%fused_computation.22 | convolution fusion | flops 134742016 | bytes 3145728 | tf_op jit(solution)/shard_map/ijnac,ijndc->ijnad/dot_general | solution.py:97
  121.6 3.8 fusion.3
  125.4 4.8 %convert_bitcast_fusion.1 = bf16[4,4,3,512,128]{3,4,1,2,0:T(8,128)(2,1)S(1)} fusion(bf16[4,4,3,256,128]{4,3,2,1,0:T(8,128)(2,1)} %get-tuple-element.12, bf16[4,3,512,256,1]{3,0,2,1,4:T(4,128)(2,1)} %bitcast.64), kind=kOutput, calls=%fused_computation.6 | convolution fusion | flops 1613758464 | bytes 12582912 | tf_op jit(solution)/shard_map/isap,ijspq->ijsaq/dot_general | solution.py:53
  130.2 0.4 fusion.64
  130.7 1.8 fusion.22
  132.4 235.9 %all-gather.6.cloned.1.call-done = bf16[64,3,512,256]{3,2,1,0:T(8,128)(2,1)} async-done(((bf16[4,3,512,256]{3,2,1,0:T(8,128)(2,1)}), bf16[64,3,512,256]{3,2,1,0:T(8,128)(2,1)}) %all-gather.6.cloned.1.call-update) | async-done | bytes 50331664 | tf_op jit(solution)/shard_map/all_gather | solution.py:14
  368.3 16.9 %reduce_sum.12 = bf16[4,3,512,256]{3,2,1,0:T(8,128)(2,1)S(1)} reduce(bf16[16,4,3,512,256]{4,3,2,1,0:T(8,128)(2,1)} %bitcast.62, bf16[]{:T(256)} %constant.60.clone.1), dimensions={0}, to_apply=%region_0.1 | reduce | flops 23592960 | bytes 53477376 | tf_op jit(solution)/shard_map/reduce_sum | solution.py:14
  385.3 2.4 copy.174
  387.7 1.8 convert_bitcast_fusion
  389.6 0.4 fusion.62
  390.1 0.5 copy-done.2
  390.6 0.2 copy-done.3
  390.8 0.2 copy-done.9
  391.0 1.0 fusion.52
  392.0 0.9 reshape.46
  (28 shorter events, 0.2 us)
Async XLA Ops:
  6.5 62.7 %all-gather.4.cloned.1.call-start = ((), (), s32[]{:S(2)}) async-start(), calls=%async_computation | async-start | bytes 8912896 | tf_op jit(solution)/shard_map/all_gather | solution.py:46
  7.3 361.1 %all-gather.6.cloned.1.call-start = ((), (), s32[]{:S(2)}) async-start(), calls=%async_computation.1 | async-start | bytes 53477376 | tf_op jit(solution)/shard_map/all_gather | solution.py:14
  82.4 0.9 copy-start.1
  82.4 12.1 %copy-start.5 = (s32[64,4]{0,1:T(4,128)S(1)}, s32[64,4]{0,1:T(4,128)}, u32[]{:S(2)}) copy-start(s32[64,4]{0,1:T(4,128)} %param.18) | copy-start | bytes 3076
  82.4 12.5 %copy-start.4 = (f32[64,4]{0,1:T(4,128)S(1)}, f32[64,4]{0,1:T(4,128)}, u32[]{:S(2)}) copy-start(f32[64,4]{0,1:T(4,128)} %param.19) | copy-start | bytes 3076
  82.4 12.6 %copy-start.7 = (s32[4,4]{1,0:T(4,128)S(1)}, s32[4,4]{1,0:T(4,128)}, u32[]{:S(2)}) copy-start(s32[4,4]{1,0:T(4,128)} %param.16) | copy-start | bytes 196
  83.4 23.7 %collective-permute-start.3 = (bf16[4,4,4096]{2,0,1:T(4,128)(2,1)S(1)}, bf16[4,4,4096]{2,0,1:T(4,128)(2,1)S(1)}, u32[]{:S(2)}, u32[]{:S(2)}) collective-permute-start(bf16[4,4,4096]{2,0,1:T(4,128)(2,1)S(1)} %copy.84), channel_id=1, source_target_pairs={{1,0},{2,1},{3,2},{4,3},{5,4},{6,5},{7,6},{8,7},{9,8},{10,9},{11,1... | collective-permute-start | bytes 393224 | tf_op jit(solution)/shard_map/ppermute | solution.py:20
  85.6 21.5 %collective-permute-start.2 = (bf16[4,4,4096]{2,0,1:T(4,128)(2,1)S(1)}, bf16[4,4,4096]{2,0,1:T(4,128)(2,1)S(1)}, u32[]{:S(2)}, u32[]{:S(2)}) collective-permute-start(bf16[4,4,4096]{2,0,1:T(4,128)(2,1)S(1)} %copy.84), channel_id=1, source_target_pairs={{0,1},{1,2},{2,3},{3,4},{4,5},{5,6},{6,7},{7,8},{8,9},{9,10},{10,1... | collective-permute-start | bytes 393224 | tf_op jit(solution)/shard_map/ppermute | solution.py:20
  89.0 19.4 %collective-permute-start.1 = (bf16[4,4,4096]{2,1,0:T(4,128)(2,1)S(1)}, bf16[4,4,4096]{2,1,0:T(4,128)(2,1)S(1)}, u32[]{:S(2)}, u32[]{:S(2)}) collective-permute-start(bf16[4,4,4096]{2,1,0:T(4,128)(2,1)S(1)} %copy-done.1), channel_id=1, source_target_pairs={{16,0},{32,16},{48,32},{64,48},{80,64},{96,80},{112,96},{128,112},... | collective-permute-start | bytes 393224 | tf_op jit(solution)/shard_map/ppermute | solution.py:20
  90.3 18.1 %collective-permute-start = (bf16[4,4,4096]{2,1,0:T(4,128)(2,1)S(1)}, bf16[4,4,4096]{2,1,0:T(4,128)(2,1)S(1)}, u32[]{:S(2)}, u32[]{:S(2)}) collective-permute-start(bf16[4,4,4096]{2,1,0:T(4,128)(2,1)S(1)} %copy-done.1), channel_id=1, source_target_pairs={{0,16},{16,32},{32,48},{48,64},{64,80},{80,96},{96,112},{112,128},... | collective-permute-start | bytes 393224 | tf_op jit(solution)/shard_map/ppermute | solution.py:20
  95.1 7.1 %copy-start.6 = (f32[64]{0:T(128)S(1)}, f32[64]{0:T(128)}, u32[]{:S(2)}) copy-start(f32[64]{0:T(128)} %param.15) | copy-start | bytes 772
  385.3 2.4 copy-start
  389.6 1.0 copy-start.2
  389.6 1.2 copy-start.3
  389.6 1.2 copy-start.8
  389.6 1.3 copy-start.9
Sparse Core Ops, SparseCore 0:
  9.2 60.0 all-gather.3
  82.6 285.7 all-gather.5
